TPU v7x, 256 devices: a whole 4x4x8 slice. The times are simulated.
256 devices in a mesh: tm: 64 (over z, x, core), row: 4 (over y).
Axes of the slice: x: 4, y: 4, z: 8, core: 2. Of those that a mesh axis runs over, the one named last changes fastest.
Arguments:
- filter_map: bfloat16 [1024, 256, 256], P('tm', 'row'), may hold values from -1 to 1
- filter_cov: bfloat16 [1024, 256, 256], P('tm', 'row'), may hold values from -1 to 1
- smoother_gain: bfloat16 [1024, 256, 256], P('tm', 'row'), may hold values from -1 to 1
- transition: bfloat16 [256, 256], replicated, may hold values from -0.375 to 0.375
- site_basis: bfloat16 [2048, 256], replicated, may hold values from -0.375 to 0.375
- obs_time: int32 [32768], P('tm'), may hold values from 0 to 1023, as said below
- obs_site: int32 [32768], P('tm'), may hold values from 0 to 2047
- obs_value: float32 [32768, 128], P('tm'), may hold values from -6 to 6
- obs_weight: float32 [32768], P('tm'), may hold values from 0.5 to 8
Outputs:
- smoothed: float32 [1024, 256, 128], P('tm', 'row')
Inputs may be any that keep to these rules, and one draw needn't show every extreme that they name: `obs_time`: row r has a time step from (r // 512) * 16 to (r // 512 + 1) * 16 - 1; rows are in no order of time.
All inputs are finite; a program needn't handle non-finite values.
Results may differ from a plain program's by a relative error of at most 0.0041.
Values may be sent and summed in bfloat16 or wider, within the bound.
No kernel may reach another device: no remote copies, remote signals or barrier semaphores. Data moves between devices by JAX's collectives and lax.ppermute only.
A program may use at most 128 MiB of HBM per device.

v0:
```python
import jax
import jax.numpy as jnp
from jax import lax
from jax.sharding import PartitionSpec as P

highest = lax.Precision.HIGHEST


def entering(value, axis, join, neutral, backward):
    count, mine = (lax.axis_size(axis), lax.axis_index(axis))
    pieces = jax.tree.map(lambda part: lax.all_gather(part, axis), value)
    if backward:
        pieces = jax.tree.map(lambda part: part[::-1], pieces)
        mine = count - 1 - mine
    running = jax.tree.map(
        lambda part, zero: jnp.full_like(part, 0) + jnp.asarray(zero, part.dtype), value, neutral
    )

    def step(position, running):
        longer = join(running, jax.tree.map(lambda part: part[position], pieces))
        return jax.tree.map(lambda new, old: jnp.where(position < mine, new, old), longer, running)

    return lax.fori_loop(0, count - 1, step, running)


def product(first_factor, second_factor):
    return jnp.dot(
        first_factor, second_factor, precision=highest, preferred_element_type=jnp.float32
    )


def compose(earlier, later):
    return (product(later[0], earlier[0]), product(later[0], earlier[1]) + later[1])


def gain_at(gain_matrix, last_flag):
    return jnp.where(last_flag, jnp.zeros((), jnp.float32), gain_matrix.astype(jnp.float32))


def build_information(obs_time, obs_site, obs_value, obs_weight, site_basis, num_steps):
    local_time = obs_time - lax.axis_index("tm") * num_steps
    basis_rows = jnp.take(site_basis, obs_site, axis=0)
    weighted = (obs_weight[:, None] * obs_value).astype(jnp.bfloat16)

    def one_step(time_step_index):
        masked = jnp.where(
            (local_time == time_step_index)[:, None], basis_rows, jnp.zeros((), jnp.bfloat16)
        )
        summed = lax.dot_general(
            masked, weighted, (((0,), (0,)), ((), ())), preferred_element_type=jnp.float32
        )
        return summed.astype(jnp.bfloat16)

    return lax.map(one_step, jnp.arange(num_steps, dtype=jnp.int32))


def forward_prefix(summary, identity_pair):
    return entering((summary[0], summary[1]), "tm", compose, identity_pair, False)


def backward_prefix(summary, identity_pair):
    return entering((summary[0], summary[1]), "tm", compose, identity_pair, True)


def offset_terms(gains, mean_share, filtered, transition_wide, final_flags):

    def one_offset(running, inputs):
        gain_matrix, mean_part, mean_whole, last_flag = inputs
        pushed = product(transition_wide, mean_whole)
        corrected = mean_part - product(gain_at(gain_matrix, last_flag), pushed)
        return (running, jnp.where(last_flag, mean_part, corrected))

    return lax.scan(one_offset, 0, (gains, mean_share, filtered, final_flags))[1]


def whole_passes(maps_whole, gains_whole, drive_whole, transition_wide, final_flags, identity_pair):

    def summary_step(running, inputs):
        return (compose(running, (inputs[0].astype(jnp.float32), inputs[1])), None)

    summary = lax.scan(summary_step, identity_pair, (maps_whole, drive_whole))[0]
    incoming = forward_prefix(summary, identity_pair)

    def filter_step(current, inputs):
        current = product(inputs[0].astype(jnp.float32), current) + inputs[1]
        return (current, current)

    filtered = lax.scan(filter_step, incoming[1], (maps_whole, drive_whole))[1]
    offsets = offset_terms(gains_whole, filtered, filtered, transition_wide, final_flags)

    def smooth_summary(running, inputs):
        return (compose(running, (gain_at(inputs[0], inputs[2]), inputs[1])), None)

    back_summary = lax.scan(
        smooth_summary, identity_pair, (gains_whole, offsets, final_flags), reverse=True
    )[0]
    outgoing = backward_prefix(back_summary, identity_pair)

    def smooth_step(current, inputs):
        current = product(gain_at(inputs[0], inputs[2]), current) + inputs[1]
        return (current, current)

    return lax.scan(smooth_step, outgoing[1], (gains_whole, offsets, final_flags), reverse=True)[1]


def local(
    filter_map,
    filter_cov,
    smoother_gain,
    transition,
    site_basis,
    obs_time,
    obs_site,
    obs_value,
    obs_weight,
):
    num_steps = filter_map.shape[0]
    row_count = filter_map.shape[1]
    state_width = filter_map.shape[2]
    members = obs_value.shape[1]
    row_start = lax.axis_index("row") * row_count
    is_final = lax.axis_index("tm") == lax.axis_size("tm") - 1
    final_flags = jnp.logical_and(is_final, jnp.arange(num_steps) == num_steps - 1)
    identity = jnp.eye(state_width, dtype=jnp.float32)
    transition_wide = transition.astype(jnp.float32)
    identity_pair = (identity, jnp.zeros((state_width, members), jnp.float32))
    information = build_information(
        obs_time, obs_site, obs_value, obs_weight, site_basis, num_steps
    )
    maps_whole, gains_whole, covs_whole = (
        lax.all_gather(filter_map, "row", axis=1, tiled=True),
        lax.all_gather(smoother_gain, "row", axis=1, tiled=True),
        lax.all_gather(filter_cov, "row", axis=1, tiled=True),
    )
    drive_whole = jnp.einsum(
        "kij,kje->kie", covs_whole, information, preferred_element_type=jnp.float32
    )
    smoothed = whole_passes(
        maps_whole, gains_whole, drive_whole, transition_wide, final_flags, identity_pair
    )
    return lax.dynamic_slice_in_dim(smoothed, row_start, row_count, 1)


def solution(mesh):
    placed = (
        P("tm", "row", None),
        P("tm", "row", None),
        P("tm", "row", None),
        P(),
        P(),
        P("tm"),
        P("tm"),
        P("tm", None),
        P("tm"),
    )
    return jax.shard_map(
        local, mesh=mesh, in_specs=placed, out_specs=P("tm", "row", None), check_vma=False
    )
```

profile of v0, /device:TPU:1, one launch (start us, length us, event | category | flops | bytes accessed | tf_op | source)
XLA Modules:
  0.0 877.9 jit_solution(3602552848383626959)
XLA Ops:
  12.4 38.2 %while.106 = (s32[]{:T(128)}, bf16[16,256,128]{2,1,0:T(8,128)(2,1)}, s32[16]{0:T(128)S(1)}, s32[512]{0:T(512)S(1)}, bf16[512,256]{1,0:T(8,128)(2,1)S(1)}, /*index=5*/bf16[512,128]{1,0:T(8,128)(2,1)S(1)}, s32[]{:T(128)}) while((s32[]{:T(128)}, bf16[16,256,128]{2,1,0:T(8,128)(2,1)}, s32[16]{0:T(128)S(1)}, s32[512]{0:T(512)S(1)}, ...), condition=%wide.region_1.2_spmd, body=%wide.region_0.1_spmd.sunk | while | flops 33718784 | bytes 462429 | solution.py:54
  50.7 2.7 convolution_bitcast_fusion
  55.3 26.1 %all-gather.14.cloned.1.call-done = bf16[16,256,256]{2,1,0:T(8,128)(2,1)} async-done(((bf16[16,64,256]{2,1,0:T(8,128)(2,1)}), bf16[16,256,256]{2,1,0:T(8,128)(2,1)}) %all-gather.14.cloned.1.call-update) | async-done | bytes 2097168 | tf_op jit(solution)/shard_map/all_gather | solution.py:131
  81.4 40.7 %while.110 = (s32[]{:T(128)}, f32[256,256]{1,0:T(8,128)S(1)}, f32[256,128]{1,0:T(8,128)S(1)}, bf16[16,256,256]{2,1,0:T(8,128)(2,1)}, f32[16,256,128]{2,1,0:T(8,128)}, /*index=5*/s32[]{:T(128)}, s32[]{:T(128)}) while((s32[]{:T(128)}, f32[256,256]{1,0:T(8,128)S(1)}, f32[256,128]{1,0:T(8,128)S(1)}, bf16[16,256,256]{2,1,0:T(8,128)(2,1)}, ...), condition=%wide.region_3.4_spmd.clone, body=%wide.region_2.3_spmd.clone.sunk | while | flops 302055424 | bytes 1967703 | solution.py:81
  124.1 82.4 %all-gather.20.cloned.1.call-done = f32[16384,128]{1,0:T(8,128)} async-done(((f32[256,128]{1,0:T(8,128)}), f32[16384,128]{1,0:T(8,128)}) %all-gather.20.cloned.1.call-update) | async-done | bytes 8388624 | tf_op jit(solution)/shard_map/all_gather | solution.py:11
  206.5 98.7 %all-gather.18.cloned.1.call-done = f32[16384,256]{1,0:T(8,128)} async-done(((f32[256,256]{1,0:T(8,128)}), f32[16384,256]{1,0:T(8,128)}) %all-gather.18.cloned.1.call-update) | async-done | bytes 16777232 | tf_op jit(solution)/shard_map/all_gather | solution.py:11
  305.2 89.4 %while.111 = (s32[]{:T(128)}, f32[256,128]{1,0:T(8,128)S(1)}, s32[]{:T(128)}, f32[64,256,256]{2,1,0:T(8,128)}, f32[64,256,128]{2,1,0:T(8,128)}, /*index=5*/s32[]{:T(128)}, s32[]{:T(128)}) while((s32[]{:T(128)}, f32[256,128]{1,0:T(8,128)S(1)}, s32[]{:T(128)}, f32[64,256,256]{2,1,0:T(8,128)}, f32[64,256,128]{2,1,0:T(8,128)}, ...), condition=%wide.region_5.6_spmd.clone, body=%wide.region_4.5_spmd.clone.sunk | while | flops 100794368 | bytes 1051231 | solution.py:23
  394.7 20.7 %while.107 = (s32[]{:T(128)}, f32[256,128]{1,0:T(8,128)S(1)}, f32[16,256,128]{2,1,0:T(8,128)S(1)}, bf16[16,256,256]{2,1,0:T(8,128)(2,1)}, f32[16,256,128]{2,1,0:T(8,128)}, /*index=5*/s32[]{:T(128)}) while((s32[]{:T(128)}, f32[256,128]{1,0:T(8,128)S(1)}, f32[16,256,128]{2,1,0:T(8,128)S(1)}, bf16[16,256,256]{2,1,0:T(8,128)(2,1)}, ...), condition=%wide.region_7.8_spmd, body=%wide.region_6.7_spmd.sunk | while | flops 100696064 | bytes 918597 | solution.py:88
  417.0 57.1 %while.108 = (s32[]{:T(128)}, f32[16,256,128]{2,1,0:T(8,128)}, pred[16]{0:T(512)(128)(4,1)S(1)}, f32[16,256,128]{2,1,0:T(8,128)S(1)}, bf16[16,256,256]{2,1,0:T(8,128)(2,1)}, /*index=5*/f32[256,256]{1,0:T(8,128)S(1)}, s32[]{:T(128)}) while((s32[]{:T(128)}, f32[16,256,128]{2,1,0:T(8,128)}, pred[16]{0:T(512)(128)(4,1)S(1)}, ...), condition=%wide.region_9.10_spmd, body=%wide.region_8.9_spmd.sunk | while | flops 201523200 | bytes 1050711 | solution.py:73
  418.0 2.6 fusion.121
  421.6 2.6 fusion.121
  425.1 2.6 fusion.121
  428.7 2.6 fusion.121
  432.3 2.6 fusion.121
  435.9 2.6 fusion.121
  439.4 2.6 fusion.121
  443.0 2.6 fusion.121
  446.6 2.6 fusion.121
  450.2 2.6 fusion.121
  453.7 2.6 fusion.121
  457.3 2.6 fusion.121
  460.8 2.6 fusion.121
  464.4 2.6 fusion.121
  468.0 2.6 fusion.121
  471.5 2.6 fusion.121
  474.1 73.4 %while.112 = (s32[]{:T(128)}, f32[256,256]{1,0:T(8,128)S(1)}, f32[256,128]{1,0:T(8,128)S(1)}, pred[16]{0:T(512)(128)(4,1)S(1)}, bf16[16,256,256]{2,1,0:T(8,128)(...) while((s32[]{:T(128)}, f32[256,256]{1,0:T(8,128)S(1)}, ...), condition=%wide.region_11.12_spmd.clone, body=%wide.region_10.11_spmd.clone.sunk | while | flops 302317568 | bytes 1968764 | solution.py:94
  474.7 2.0 convolution_add_fusion.9
  479.3 2.0 convolution_add_fusion.9
  549.0 79.4 %all-gather.24.cloned.1.call-done = f32[16384,128]{1,0:T(8,128)} async-done(((f32[256,128]{1,0:T(8,128)}), f32[16384,128]{1,0:T(8,128)}) %all-gather.24.cloned.1.call-update) | async-done | bytes 8388624 | tf_op jit(solution)/shard_map/all_gather | solution.py:11
  628.3 7.6 rev.7
  636.0 91.2 %all-gather.22.cloned.1.call-done = f32[16384,256]{1,0:T(8,128)} async-done(((f32[256,256]{1,0:T(8,128)}), f32[16384,256]{1,0:T(8,128)}) %all-gather.22.cloned.1.call-update) | async-done | bytes 16777232 | tf_op jit(solution)/shard_map/all_gather | solution.py:11
  727.2 11.5 %rev.6 = f32[64,256,256]{2,1,0:T(8,128)} reverse(f32[64,256,256]{2,1,0:T(8,128)} %bitcast.136), dimensions={0} | reverse | bytes 33554432 | tf_op jit(solution)/shard_map/rev | solution.py:13
  738.7 89.4 %while.113 = (s32[]{:T(128)}, f32[256,128]{1,0:T(8,128)S(1)}, s32[]{:T(128)}, f32[64,256,256]{2,1,0:T(8,128)}, f32[64,256,128]{2,1,0:T(8,128)}, /*index=5*/s32[]{:T(128)}, s32[]{:T(128)}) while((s32[]{:T(128)}, f32[256,128]{1,0:T(8,128)S(1)}, s32[]{:T(128)}, f32[64,256,256]{2,1,0:T(8,128)}, f32[64,256,128]{2,1,0:T(8,128)}, ...), condition=%wide.region_13.14_spmd.clone, body=%wide.region_12.13_spmd.clone.sunk | while | flops 100794368 | bytes 1051231 | solution.py:23
  828.3 41.9 %while.109 = (s32[]{:T(128)}, f32[256,128]{1,0:T(8,128)S(1)}, f32[16,256,128]{2,1,0:T(8,128)S(1)}, pred[16]{0:T(512)(128)(4,1)S(1)}, bf16[16,256,256]{2,1,0:T(8,...) while((s32[]{:T(128)}, f32[256,128]{1,0:T(8,128)S(1)}, f32[16,256,128]{2,1,0:T(8,128)S(1)}, ...), condition=%wide.region_15.16_spmd, body=%wide.region_14.15_spmd.sunk | while | flops 100827136 | bytes 919143 | solution.py:103
  828.9 2.0 bitcast_dynamic-update-slice_fusion.5
  831.5 2.0 bitcast_dynamic-update-slice_fusion.5
  834.1 2.0 bitcast_dynamic-update-slice_fusion.5
  836.8 2.0 bitcast_dynamic-update-slice_fusion.5
  839.4 2.0 bitcast_dynamic-update-slice_fusion.5
  842.0 2.0 bitcast_dynamic-update-slice_fusion.5
  844.6 2.0 bitcast_dynamic-update-slice_fusion.5
  847.2 2.0 bitcast_dynamic-update-slice_fusion.5
  849.9 2.0 bitcast_dynamic-update-slice_fusion.5
  852.5 2.0 bitcast_dynamic-update-slice_fusion.5
  855.1 2.0 bitcast_dynamic-update-slice_fusion.5
  857.7 2.0 bitcast_dynamic-update-slice_fusion.5
  860.3 2.0 bitcast_dynamic-update-slice_fusion.5
  865.6 2.0 bitcast_dynamic-update-slice_fusion.5
  (596 shorter events, 384.2 us)
Async XLA Ops:
  6.5 3.6 copy-start
  6.5 5.7 copy-start.6
  6.5 5.7 copy-start.8
  6.5 44.1 %all-gather.16.cloned.1.call-start = ((), (), s32[]{:S(2)}) async-start(), calls=%async_computation.2 | async-start | bytes 2621440 | tf_op jit(solution)/shard_map/all_gather | solution.py:133
  7.3 74.1 %all-gather.14.cloned.1.call-start = ((), (), s32[]{:S(2)}) async-start(), calls=%async_computation.1 | async-start | bytes 2621440 | tf_op jit(solution)/shard_map/all_gather | solution.py:131
  8.0 198.5 %all-gather.20.cloned.1.call-start = ((), (), s32[]{:S(2)}) async-start(), calls=%async_computation.4 | async-start | bytes 8519680 | tf_op jit(solution)/shard_map/all_gather | solution.py:11
  81.4 42.6 %copy-start.7 = (bf16[256,256]{1,0:T(8,128)(2,1)S(1)}, bf16[256,256]{1,0:T(8,128)(2,1)}, u32[]{:S(2)}) copy-start(bf16[256,256]{1,0:T(8,128)(2,1)} %param.28) | copy-start | bytes 393220
  122.1 0.7 copy-start.5
  122.1 0.7 copy-start.3
  122.8 182.4 %all-gather.18.cloned.1.call-start = ((), (), s32[]{:S(2)}) async-start(), calls=%async_computation.3 | async-start | bytes 17039360 | tf_op jit(solution)/shard_map/all_gather | solution.py:11
  123.4 292.1 %all-gather.12.cloned.1.call-start = ((), (), s32[]{:S(2)}) async-start(), calls=%async_computation | async-start | bytes 2621440 | tf_op jit(solution)/shard_map/all_gather | solution.py:132
  123.9 504.4 %all-gather.24.cloned.1.call-start = ((), (), s32[]{:S(2)}) async-start(), calls=%async_computation.6 | async-start | bytes 8519680 | tf_op jit(solution)/shard_map/all_gather | solution.py:11
  547.5 0.7 copy-start.4
  547.6 0.7 copy-start.2
  548.2 178.9 %all-gather.22.cloned.1.call-start = ((), (), s32[]{:S(2)}) async-start(), calls=%async_computation.5 | async-start | bytes 17039360 | tf_op jit(solution)/shard_map/all_gather | solution.py:11
  828.3 42.8 %copy-start.1 = (bf16[2048,256]{1,0:T(8,128)(2,1)S(1)}, bf16[2048,256]{1,0:T(8,128)(2,1)}, u32[]{:S(2)}) copy-start(bf16[2048,256]{1,0:T(8,128)(2,1)} %param.29) | copy-start | bytes 3145732
Sparse Core Ops, SparseCore 0:
  9.1 36.9 all-gather.15
  48.0 33.3 all-gather.13
  122.9 83.5 all-gather.19
  209.1 96.0 all-gather.17
  306.8 29.7 all-gather.11
  548.3 79.9 all-gather.23
  631.1 96.0 all-gather.21
where the time goes:
time: 883 us; the launch traced here: 878 us
  matrix products  394 us (45%)
  waiting for transfers between devices  381 us (43%)
  local copies, waits for them, and re-layouts  68.6 us (8%)
  between operations  13.8 us (2%)
  other arithmetic  13.5 us (2%)
    dot_general x254, matrix products, product(): jnp.dot(first_factor, second_factor, precision=highest, preferred_element...  375 us
    all_gather x4, waiting for transfers between devices, entering(): pieces = jax.tree.map(lambda part: lax.all_gather(part, axis), value)  352 us
    dynamic_slice x48, local copies, waits for them, and re-layouts, offset_terms(): lax.scan(one_offset, 0, (gains, mean_share, filtered, final_flags))[1]  28.3 us
    all_gather x1, waiting for transfers between devices, local(): lax.all_gather(filter_map, 'row', axis=1, tiled=True)  26.1 us
    rev x2, local copies, waits for them, and re-layouts, entering(): pieces = jax.tree.map(lambda part: part[::-1], pieces)  19.1 us
  transfers between devices with their start and end apart: 7, of which 5 were waited for; matrix products, arithmetic and copies ran while one was open for 18% of the time, Pallas kernels for 0%

commit v1 on v0

--- a/solution.py
+++ b/solution.py
@@ -128,7 +128,9 @@
         obs_time, obs_site, obs_value, obs_weight, site_basis, num_steps
     )
     maps_whole, gains_whole, covs_whole = (
-        lax.all_gather(filter_map, "row", axis=1, tiled=True),
+        jnp.concatenate(
+            lax.all_to_all(jnp.stack([filter_map] * lax.axis_size("row")), "row", 0, 0), axis=1
+        ),
         lax.all_gather(smoother_gain, "row", axis=1, tiled=True),
         lax.all_gather(filter_cov, "row", axis=1, tiled=True),
     )

time: 883 us -> 868 us (0.983)
  waiting for transfers between devices: 381 us -> 358 us
    all_gather x1 -> x0, waiting for transfers between devices: 26.1 us -> none  [local(): lax.all_gather(filter_map, 'row', axis=1, tiled=True)]
  transfers between devices with their start and end apart: 7 -> 7, of which waited for: 5 -> 5; matrix products, arithmetic and copies ran while one was open for 18% -> 19% of each run, Pallas kernels for 0% -> 0%
where the time goes in v1:
time: 868 us; the launch traced here: 863 us
  matrix products  394 us (45%)
  waiting for transfers between devices  358 us (41%)
  local copies, waits for them, and re-layouts  72.7 us (8%)
  between operations  13.8 us (2%)
  other arithmetic  12.4 us (1%)
    dot_general x254, matrix products, product(): jnp.dot(first_factor, second_factor, precision=highest, preferred_element...  375 us
    all_gather x4, waiting for transfers between devices, entering(): pieces = jax.tree.map(lambda part: lax.all_gather(part, axis), value)  354 us
    dynamic_slice x48, local copies, waits for them, and re-layouts, offset_terms(): lax.scan(one_offset, 0, (gains, mean_share, filtered, final_flags))[1]  28.3 us
    rev x2, local copies, waits for them, and re-layouts, entering(): pieces = jax.tree.map(lambda part: part[::-1], pieces)  19.1 us
  transfers between devices with their start and end apart: 7, of which 5 were waited for; matrix products, arithmetic and copies ran while one was open for 19% of the time, Pallas kernels for 0%

profile of v1, /device:TPU:1, one launch (start us, length us, event | category | flops | bytes accessed | tf_op | source)
XLA Modules:
  0.0 862.5 jit_solution(12235916507256894046)
XLA Ops:
  7.3 2.6 stack.2
  9.9 5.1 all-to-all-start
  18.3 38.1 %while.106 = (s32[]{:T(128)}, bf16[16,256,128]{2,1,0:T(8,128)(2,1)}, s32[16]{0:T(128)S(1)}, s32[512]{0:T(512)S(1)}, bf16[512,256]{1,0:T(8,128)(2,1)S(1)}, /*index=5*/bf16[512,128]{1,0:T(8,128)(2,1)S(1)}, s32[]{:T(128)}) while((s32[]{:T(128)}, bf16[16,256,128]{2,1,0:T(8,128)(2,1)}, s32[16]{0:T(128)S(1)}, s32[512]{0:T(512)S(1)}, ...), condition=%wide.region_1.2_spmd, body=%wide.region_0.1_spmd.sunk | while | flops 33718784 | bytes 462429 | solution.py:54
  58.7 2.7 convolution_bitcast_fusion
  63.3 40.7 %while.110 = (s32[]{:T(128)}, f32[256,256]{1,0:T(8,128)S(1)}, f32[256,128]{1,0:T(8,128)S(1)}, bf16[16,256,256]{2,1,0:T(8,128)(2,1)}, f32[16,256,128]{2,1,0:T(8,128)}, /*index=5*/s32[]{:T(128)}, s32[]{:T(128)}) while((s32[]{:T(128)}, f32[256,256]{1,0:T(8,128)S(1)}, f32[256,128]{1,0:T(8,128)S(1)}, bf16[16,256,256]{2,1,0:T(8,128)(2,1)}, ...), condition=%wide.region_3.4_spmd.clone, body=%wide.region_2.3_spmd.clone.sunk | while | flops 302055424 | bytes 1967703 | solution.py:81
  106.1 85.0 %all-gather.17.cloned.1.call-done = f32[16384,128]{1,0:T(8,128)} async-done(((f32[256,128]{1,0:T(8,128)}), f32[16384,128]{1,0:T(8,128)}) %all-gather.17.cloned.1.call-update) | async-done | bytes 8388624 | tf_op jit(solution)/shard_map/all_gather | solution.py:11
  191.1 98.8 %all-gather.15.cloned.1.call-done = f32[16384,256]{1,0:T(8,128)} async-done(((f32[256,256]{1,0:T(8,128)}), f32[16384,256]{1,0:T(8,128)}) %all-gather.15.cloned.1.call-update) | async-done | bytes 16777232 | tf_op jit(solution)/shard_map/all_gather | solution.py:11
  289.9 89.4 %while.111 = (s32[]{:T(128)}, f32[256,128]{1,0:T(8,128)S(1)}, s32[]{:T(128)}, f32[64,256,256]{2,1,0:T(8,128)}, f32[64,256,128]{2,1,0:T(8,128)}, /*index=5*/s32[]{:T(128)}, s32[]{:T(128)}) while((s32[]{:T(128)}, f32[256,128]{1,0:T(8,128)S(1)}, s32[]{:T(128)}, f32[64,256,256]{2,1,0:T(8,128)}, f32[64,256,128]{2,1,0:T(8,128)}, ...), condition=%wide.region_5.6_spmd.clone, body=%wide.region_4.5_spmd.clone.sunk | while | flops 100794368 | bytes 1051231 | solution.py:23
  379.5 20.7 %while.107 = (s32[]{:T(128)}, f32[256,128]{1,0:T(8,128)S(1)}, f32[16,256,128]{2,1,0:T(8,128)S(1)}, bf16[16,256,256]{2,1,0:T(8,128)(2,1)}, f32[16,256,128]{2,1,0:T(8,128)}, /*index=5*/s32[]{:T(128)}) while((s32[]{:T(128)}, f32[256,128]{1,0:T(8,128)S(1)}, f32[16,256,128]{2,1,0:T(8,128)S(1)}, bf16[16,256,256]{2,1,0:T(8,128)(2,1)}, ...), condition=%wide.region_7.8_spmd, body=%wide.region_6.7_spmd.sunk | while | flops 100696064 | bytes 918597 | solution.py:88
  401.8 57.1 %while.108 = (s32[]{:T(128)}, f32[16,256,128]{2,1,0:T(8,128)}, pred[16]{0:T(512)(128)(4,1)S(1)}, f32[16,256,128]{2,1,0:T(8,128)S(1)}, bf16[16,256,256]{2,1,0:T(8,128)(2,1)}, /*index=5*/f32[256,256]{1,0:T(8,128)S(1)}, s32[]{:T(128)}) while((s32[]{:T(128)}, f32[16,256,128]{2,1,0:T(8,128)}, pred[16]{0:T(512)(128)(4,1)S(1)}, ...), condition=%wide.region_9.10_spmd, body=%wide.region_8.9_spmd.sunk | while | flops 201523200 | bytes 1050711 | solution.py:73
  402.8 2.6 fusion.121
  406.3 2.6 fusion.121
  409.9 2.6 fusion.121
  413.5 2.6 fusion.121
  417.1 2.6 fusion.121
  420.6 2.6 fusion.121
  424.2 2.6 fusion.121
  427.8 2.6 fusion.121
  431.4 2.6 fusion.121
  434.9 2.6 fusion.121
  438.5 2.6 fusion.121
  442.1 2.6 fusion.121
  445.6 2.6 fusion.121
  449.2 2.6 fusion.121
  452.8 2.6 fusion.121
  456.3 2.6 fusion.121
  458.9 73.4 %while.112 = (s32[]{:T(128)}, f32[256,256]{1,0:T(8,128)S(1)}, f32[256,128]{1,0:T(8,128)S(1)}, pred[16]{0:T(512)(128)(4,1)S(1)}, bf16[16,256,256]{2,1,0:T(8,128)(...) while((s32[]{:T(128)}, f32[256,256]{1,0:T(8,128)S(1)}, ...), condition=%wide.region_11.12_spmd.clone, body=%wide.region_10.11_spmd.clone.sunk | while | flops 302317568 | bytes 1968764 | solution.py:94
  459.5 2.0 convolution_add_fusion.9
  464.1 2.0 convolution_add_fusion.9
  533.6 79.5 %all-gather.21.cloned.1.call-done = f32[16384,128]{1,0:T(8,128)} async-done(((f32[256,128]{1,0:T(8,128)}), f32[16384,128]{1,0:T(8,128)}) %all-gather.21.cloned.1.call-update) | async-done | bytes 8388624 | tf_op jit(solution)/shard_map/all_gather | solution.py:11
  613.1 7.6 rev.7
  620.8 91.1 %all-gather.19.cloned.1.call-done = f32[16384,256]{1,0:T(8,128)} async-done(((f32[256,256]{1,0:T(8,128)}), f32[16384,256]{1,0:T(8,128)}) %all-gather.19.cloned.1.call-update) | async-done | bytes 16777232 | tf_op jit(solution)/shard_map/all_gather | solution.py:11
  711.8 11.5 %rev.6 = f32[64,256,256]{2,1,0:T(8,128)} reverse(f32[64,256,256]{2,1,0:T(8,128)} %bitcast.139), dimensions={0} | reverse | bytes 33554432 | tf_op jit(solution)/shard_map/rev | solution.py:13
  723.3 89.4 %while.113 = (s32[]{:T(128)}, f32[256,128]{1,0:T(8,128)S(1)}, s32[]{:T(128)}, f32[64,256,256]{2,1,0:T(8,128)}, f32[64,256,128]{2,1,0:T(8,128)}, /*index=5*/s32[]{:T(128)}, s32[]{:T(128)}) while((s32[]{:T(128)}, f32[256,128]{1,0:T(8,128)S(1)}, s32[]{:T(128)}, f32[64,256,256]{2,1,0:T(8,128)}, f32[64,256,128]{2,1,0:T(8,128)}, ...), condition=%wide.region_13.14_spmd.clone, body=%wide.region_12.13_spmd.clone.sunk | while | flops 100794368 | bytes 1051231 | solution.py:23
  812.9 41.9 %while.109 = (s32[]{:T(128)}, f32[256,128]{1,0:T(8,128)S(1)}, f32[16,256,128]{2,1,0:T(8,128)S(1)}, pred[16]{0:T(512)(128)(4,1)S(1)}, bf16[16,256,256]{2,1,0:T(8,...) while((s32[]{:T(128)}, f32[256,128]{1,0:T(8,128)S(1)}, f32[16,256,128]{2,1,0:T(8,128)S(1)}, ...), condition=%wide.region_15.16_spmd, body=%wide.region_14.15_spmd.sunk | while | flops 100827136 | bytes 919143 | solution.py:103
  816.2 2.0 bitcast_dynamic-update-slice_fusion.5
  818.8 2.0 bitcast_dynamic-update-slice_fusion.5
  821.4 2.0 bitcast_dynamic-update-slice_fusion.5
  824.0 2.0 bitcast_dynamic-update-slice_fusion.5
  826.6 2.0 bitcast_dynamic-update-slice_fusion.5
  829.3 2.0 bitcast_dynamic-update-slice_fusion.5
  831.9 2.0 bitcast_dynamic-update-slice_fusion.5
  834.5 2.0 bitcast_dynamic-update-slice_fusion.5
  837.1 2.0 bitcast_dynamic-update-slice_fusion.5
  839.7 2.0 bitcast_dynamic-update-slice_fusion.5
  842.3 2.0 bitcast_dynamic-update-slice_fusion.5
  845.0 2.0 bitcast_dynamic-update-slice_fusion.5
  852.8 2.0 bitcast_dynamic-update-slice_fusion.5
  (599 shorter events, 386.4 us)
Async XLA Ops:
  6.5 8.6 copy-start
  6.5 52.2 %all-gather.13.cloned.1.call-start = ((), (), s32[]{:S(2)}) async-start(), calls=%async_computation.2 | async-start | bytes 2621440 | tf_op jit(solution)/shard_map/all_gather | solution.py:135
  9.9 5.1 copy-start.7
  9.9 5.2 copy-start.9
  9.9 46.6 %all-to-all-start = ((bf16[4,16,64,256]{3,2,1,0:T(8,128)(2,1)}), bf16[4,16,64,256]{3,2,1,0:T(8,128)(2,1)S(1)}, u32[]{:S(2)}, u32[]{:S(2)}) async-start(bf16[4,16,64,256]{3,2,1,0:T(8,128)(2,1)} %stack.2), calls=%async_computation | async-start | bytes 4194304 | tf_op jit(solution)/shard_map/all_to_all | solution.py:132
  15.0 2.2 copy-start.8
  15.0 176.1 %all-gather.17.cloned.1.call-start = ((), (), s32[]{:S(2)}) async-start(), calls=%async_computation.4 | async-start | bytes 8519680 | tf_op jit(solution)/shard_map/all_gather | solution.py:11
  63.3 42.8 %copy-start.6 = (bf16[256,256]{1,0:T(8,128)(2,1)S(1)}, bf16[256,256]{1,0:T(8,128)(2,1)}, u32[]{:S(2)}) copy-start(bf16[256,256]{1,0:T(8,128)(2,1)} %param.28) | copy-start | bytes 393220
  104.0 0.7 copy-start.5
  104.0 0.7 copy-start.3
  104.7 185.2 %all-gather.15.cloned.1.call-start = ((), (), s32[]{:S(2)}) async-start(), calls=%async_computation.3 | async-start | bytes 17039360 | tf_op jit(solution)/shard_map/all_gather | solution.py:11
  105.4 294.8 %all-gather.11.cloned.1.call-start = ((), (), s32[]{:S(2)}) async-start(), calls=%async_computation.1 | async-start | bytes 2621440 | tf_op jit(solution)/shard_map/all_gather | solution.py:134
  106.0 507.1 %all-gather.21.cloned.1.call-start = ((), (), s32[]{:S(2)}) async-start(), calls=%async_computation.6 | async-start | bytes 8519680 | tf_op jit(solution)/shard_map/all_gather | solution.py:11
  532.3 0.7 copy-start.4
  532.3 0.7 copy-start.2
  533.0 178.8 %all-gather.19.cloned.1.call-start = ((), (), s32[]{:S(2)}) async-start(), calls=%async_computation.5 | async-start | bytes 17039360 | tf_op jit(solution)/shard_map/all_gather | solution.py:11
  812.9 42.8 %copy-start.1 = (bf16[2048,256]{1,0:T(8,128)(2,1)S(1)}, bf16[2048,256]{1,0:T(8,128)(2,1)}, u32[]{:S(2)}) copy-start(bf16[2048,256]{1,0:T(8,128)(2,1)} %param.29) | copy-start | bytes 3145732
Sparse Core Ops, SparseCore 0:
  9.1 49.5 all-gather.12
  104.8 86.2 all-gather.16
  193.9 96.0 all-gather.14
  291.6 29.7 all-gather.10
  533.1 79.9 all-gather.20
  615.7 96.0 all-gather.18
